TPU v7x, 32 devices: a whole 2x2x4 slice. The times are simulated.
32 devices in a mesh: seq: 8 (over y, x, core), tp: 4 (over z).
Axes of the slice: x: 2, y: 2, z: 4, core: 2. Of those that a mesh axis runs over, the one named last changes fastest.
Arguments:
- byte_states: bfloat16 [2048, 1024], P('seq'), may hold values from -6 to 6
- enc_gain: bfloat16 [1024], replicated, may hold values from 0.25 to 1.75
- enc_qkv: bfloat16 [3, 1024, 1024], P(None, None, 'tp')
- enc_proj_out: bfloat16 [1024, 1024], P('tp'), may hold values from -0.1875 to 0.1875
- starts: int32 [8, 64], P('seq'), may hold values from 0 to 2048, as said below
- counts: int32 [8], P('seq'), may hold values from 32 to 64, as said below
- lift: bfloat16 [1024, 4096], P(None, 'tp')
- cross_kv: bfloat16 [2, 1024, 4096], P(None, None, 'tp')
- latent_gain: bfloat16 [4096], replicated, may hold values from 0.25 to 1.75
- lat_qkv: bfloat16 [3, 4096, 2048], P(None, 'seq', 'tp')
- lat_proj_out: bfloat16 [2048, 4096], P('tp', 'seq'), may hold values from -0.75 to 0.75
Outputs:
- byte_out: bfloat16 [2048, 1024], P('seq')
- latent_out: bfloat16 [512, 4096], P('seq', 'tp')
Inputs may be any that keep to these rules, and one draw needn't show every extreme that they name: `starts`: row s lists in increasing order the first byte (counted over all 2048 bytes) of each patch beginning in bytes s * 256 to (s + 1) * 256 - 1, then 2048 in unused places. Byte 0 begins a patch; every row's first patch begins fewer than 8 bytes into its block, and in some row exactly 7 bytes in. counts[s] is the number of patches listed in row s of starts; some row holds 64.
All inputs are finite; a program needn't handle non-finite values.
Results may differ from a plain program's by a relative error of at most 0.018.
Values may be sent and summed in bfloat16 or wider, within the bound.
A program may use at most 128 MiB of HBM per device.

v0:
```python
import math
import jax
import jax.numpy as jnp
from jax import lax
from jax.sharding import PartitionSpec as P

EH = 64
HD = 128
WIN = 512
SPILL = 8
epsilon = 1e-05
rope_base = 500000.0
far_position = 1 << 30


def from_behind(value, axis, steps):
    count = lax.axis_size(axis)
    leading, last = (max(0, -steps), min(count, count - steps))
    return lax.ppermute(value, axis, [(source, source + steps) for source in range(leading, last)])


def prefix(value, axis, join, neutral):
    count, mine = (lax.axis_size(axis), lax.axis_index(axis))
    pieces = lax.all_gather(value, axis)
    subtotal = jnp.full_like(value, 0) + jnp.asarray(neutral, value.dtype)

    def hop(position, subtotal):
        longer = join(subtotal, pieces[position])
        return jnp.where(position < mine, longer, subtotal)

    return lax.fori_loop(0, count - 1, hop, subtotal)


def shortened(value):

    def short(part):
        return part.astype(jnp.bfloat16) if part.dtype == jnp.float32 else part

    return jax.tree.map(short, value)


def rms_scale(values, gain_row):
    mean_square = jnp.mean(values * values, axis=-1, keepdims=True)
    return values * lax.rsqrt(mean_square + epsilon) * gain_row


def masked_softmax(scores, allowed):
    scores = jnp.where(allowed, scores, -1e30)
    largest = jnp.max(scores, axis=-1, keepdims=True)
    raised = jnp.where(allowed, jnp.exp(scores - largest), 0.0)
    return raised / jnp.sum(raised, axis=-1, keepdims=True)


def rotate(values, position):
    halfway = values.shape[-1] // 2
    frequency = jnp.power(
        rope_base, -2.0 * jnp.arange(halfway, dtype=jnp.float32) / values.shape[-1]
    )
    angles = position.astype(jnp.float32)[:, None] * frequency[None, :]
    cosine = jnp.cos(angles)[:, None, :]
    sine_rows = jnp.sin(angles)[:, None, :]
    lower_half = values[..., :halfway]
    upper_half = values[..., halfway:]
    return jnp.concatenate(
        [
            lower_half * cosine - upper_half * sine_rows,
            upper_half * cosine + lower_half * sine_rows,
        ],
        axis=-1,
    )


def patch_block(extended, first_byte, end_byte, in_use, anchor, lift, cross_kv):
    columns = anchor + jnp.arange(extended.shape[0], dtype=jnp.int32)
    inside = (
        (columns[None, :] >= first_byte[:, None])
        & (columns[None, :] < end_byte[:, None])
        & in_use[:, None]
    )
    member = inside.astype(jnp.bfloat16)
    totals = jnp.dot(member, extended, preferred_element_type=jnp.float32)
    lengths = jnp.maximum(jnp.sum(inside.astype(jnp.float32), axis=1), 1.0)
    pooled = (totals / lengths[:, None]).astype(jnp.bfloat16)
    lifted = jnp.dot(pooled, lift, preferred_element_type=jnp.float32)
    key_rows = jnp.dot(extended, cross_kv[0], preferred_element_type=jnp.float32).astype(
        jnp.bfloat16
    )
    value_rows = jnp.dot(extended, cross_kv[1], preferred_element_type=jnp.float32).astype(
        jnp.bfloat16
    )
    slot_total = first_byte.shape[0]
    head_count = lifted.shape[1] // HD
    queries = lifted.astype(jnp.bfloat16).reshape(slot_total, head_count, HD)
    scores = jnp.einsum(
        "phd,khd->hpk",
        queries,
        key_rows.reshape(-1, head_count, HD),
        preferred_element_type=jnp.float32,
    ) * (1.0 / math.sqrt(HD))
    allowed = inside | (~in_use)[:, None] & (columns[None, :] == anchor)
    weights = masked_softmax(scores, allowed[None]).astype(jnp.bfloat16)
    crossed = jnp.einsum(
        "hpk,khd->phd",
        weights,
        value_rows.reshape(-1, head_count, HD),
        preferred_element_type=jnp.float32,
    )
    crossed = crossed.reshape(slot_total, head_count * HD)
    return jnp.where(in_use[:, None], lifted + crossed, 0.0).astype(jnp.bfloat16)


def add_counts(earlier, later):
    return earlier + later


def shards(
    byte_states,
    enc_gain,
    enc_qkv,
    enc_proj_out,
    starts,
    counts,
    lift,
    cross_kv,
    latent_gain,
    lat_qkv,
    lat_proj_out,
):
    byte_rows = byte_states.shape[0]
    anchor = lax.axis_index("seq") * byte_rows
    states = byte_states.astype(jnp.float32)
    normed = rms_scale(states, enc_gain.astype(jnp.float32)).astype(jnp.bfloat16)
    projected = jnp.einsum(
        "bd,idc->ibc", normed, enc_qkv, preferred_element_type=jnp.float32
    ).astype(jnp.bfloat16)
    reach_blocks = max(WIN // byte_rows, 1)
    tail_rows = min(WIN, byte_rows)
    key_parts = []
    value_parts = []
    for distance in range(reach_blocks, 0, -1):
        moved_keys, moved_values = from_behind(
            (projected[1, byte_rows - tail_rows :], projected[2, byte_rows - tail_rows :]),
            "seq",
            distance,
        )
        key_parts.append(moved_keys)
        value_parts.append(moved_values)
    key_rows = jnp.concatenate(key_parts + [projected[1]], axis=0)
    value_rows = jnp.concatenate(value_parts + [projected[2]], axis=0)
    head_count = projected.shape[2] // EH
    scores = jnp.einsum(
        "qhd,khd->hqk",
        projected[0].reshape(byte_rows, head_count, EH),
        key_rows.reshape(-1, head_count, EH),
        preferred_element_type=jnp.float32,
    ) * (1.0 / math.sqrt(EH))
    query_pos = anchor + jnp.arange(byte_rows, dtype=jnp.int32)
    key_pos = anchor - WIN + jnp.arange(WIN + byte_rows, dtype=jnp.int32)
    allowed = (
        (key_pos[None, :] <= query_pos[:, None])
        & (key_pos[None, :] > query_pos[:, None] - WIN)
        & (key_pos[None, :] >= 0)
    )
    weights = masked_softmax(scores, allowed[None]).astype(jnp.bfloat16)
    attended = jnp.einsum(
        "hqk,khd->qhd",
        weights,
        value_rows.reshape(-1, head_count, EH),
        preferred_element_type=jnp.float32,
    )
    attended = attended.reshape(byte_rows, head_count * EH).astype(jnp.bfloat16)
    blended = lax.psum(jnp.dot(attended, enc_proj_out, preferred_element_type=jnp.float32), "tp")
    encoded = (states + blended).astype(jnp.bfloat16)
    patch_count = counts[0]
    local_starts = starts[0]
    first_local = (local_starts[0:1] - anchor).astype(jnp.bfloat16)
    next_rows, next_first = from_behind((encoded[:SPILL], first_local), "seq", -1)
    next_first = next_first.astype(jnp.int32)[0]
    extended = jnp.concatenate([encoded, next_rows], axis=0)
    slot_ids = jnp.arange(local_starts.shape[0], dtype=jnp.int32)
    in_use = slot_ids < patch_count
    following = jnp.concatenate([local_starts[1:], jnp.zeros((1,), jnp.int32)])
    patch_end = jnp.where(slot_ids + 1 < patch_count, following, anchor + byte_rows + next_first)
    patches = patch_block(extended, local_starts, patch_end, in_use, anchor, lift, cross_kv)
    offset = prefix(counts, "seq", add_counts, jnp.zeros((1,), jnp.int32))[0]
    position = offset + slot_ids
    slot_total = patches.shape[0]
    full_rows = lax.all_gather(patches, "tp", axis=1, tiled=True)
    normed_rows = rms_scale(full_rows.astype(jnp.float32), latent_gain.astype(jnp.float32)).astype(
        jnp.bfloat16
    )
    inner_width = lat_qkv.shape[2]
    projected = jnp.einsum(
        "pd,idc->ipc",
        normed_rows,
        lax.all_gather(lat_qkv, "seq", axis=1, tiled=True),
        preferred_element_type=jnp.float32,
    )
    heads_here = inner_width // HD
    queries = rotate(projected[0].reshape(slot_total, heads_here, HD), position).astype(
        jnp.bfloat16
    )
    latent_keys = (
        rotate(projected[1].reshape(slot_total, heads_here, HD), position)
        .astype(jnp.bfloat16)
        .reshape(slot_total, inner_width)
    )
    latent_values = projected[2].astype(jnp.bfloat16)
    latent_pos = jnp.where(in_use, position, far_position)
    largest = jnp.full((heads_here, slot_total), -1e30, jnp.float32)
    piece_keys = lax.all_gather(latent_keys, "seq", axis=0, tiled=True)
    piece_values = lax.all_gather(latent_values, "seq", axis=0, tiled=True)
    piece_pos = lax.all_gather(shortened(latent_pos), "seq", axis=0, tiled=True)
    rows_here = piece_keys.shape[0]
    piece_scores = jnp.einsum(
        "qhd,khd->hqk",
        queries,
        piece_keys.reshape(rows_here, heads_here, HD),
        preferred_element_type=jnp.float32,
    ) * (1.0 / math.sqrt(HD))
    permitted = (piece_pos[None, :] <= position[:, None])[None]
    piece_scores = jnp.where(permitted, piece_scores, -1e30)
    renewed = jnp.maximum(largest, jnp.max(piece_scores, axis=-1))
    raised = jnp.where(permitted, jnp.exp(piece_scores - renewed[..., None]), 0.0)
    weight_sum = jnp.sum(raised, axis=-1)
    weighted = jnp.einsum(
        "hqk,khd->hqd",
        raised.astype(jnp.bfloat16),
        piece_values.reshape(rows_here, heads_here, HD),
        preferred_element_type=jnp.float32,
    )
    largest, weight_sum, weighted = (renewed, weight_sum, weighted)
    latent_heads = (
        (weighted / weight_sum[..., None])
        .transpose(1, 0, 2)
        .reshape(slot_total, inner_width)
        .astype(jnp.bfloat16)
    )
    partials = jnp.dot(
        latent_heads,
        lax.all_gather(lat_proj_out, "seq", axis=1, tiled=True),
        preferred_element_type=jnp.float32,
    )
    reduced = lax.psum_scatter(partials, "tp", scatter_dimension=1, tiled=True)
    latent = jnp.where(in_use[:, None], patches.astype(jnp.float32) + reduced, 0.0).astype(
        jnp.bfloat16
    )
    return (encoded, latent)


def solution(mesh):
    return jax.shard_map(
        shards,
        mesh=mesh,
        in_specs=(
            P("seq", None),
            P(),
            P(None, None, "tp"),
            P("tp", None),
            P("seq", None),
            P("seq"),
            P(None, "tp"),
            P(None, None, "tp"),
            P(),
            P(None, "seq", "tp"),
            P("tp", "seq"),
        ),
        out_specs=(P("seq", None), P("seq", "tp")),
        check_vma=False,
    )
```

profile of v0, /device:TPU:0, one launch (start us, length us, event | category | flops | bytes accessed | tf_op | source)
XLA Modules:
  0.0 188.4 jit_solution(6038080020906645445)
XLA Ops:
  8.1 0.8 convert_element_type.99
  8.9 1.2 fusion.40
  10.1 2.4 %fusion.30 = bf16[3,256,256]{1,2,0:T(8,128)(2,1)S(1)} fusion(bf16[3,1024,256]{2,1,0:T(8,128)(2,1)} %param.15, bf16[256,1024]{1,0:T(8,128)(2,1)} %param.13, f32[1024]{0:T(1024)S(1)} %convert_element_type.99, f32[256]{0:T(256)S(1)} %add_rsqrt_fusion), kind=kOutput, calls=%fused_computation.34 | convolution fusion | flops 403898368 | bytes 2495488 | tf_op jit(solution)/shard_map/bd,idc->ibc/dot_general | solution.py:133
  12.5 4.9 %collective-permute-start.2 = (bf16[256,256]{0,1:T(8,128)(2,1)S(1)}, bf16[256,256]{0,1:T(8,128)(2,1)S(1)}, u32[]{:S(2)}, u32[]{:S(2)}) collective-permute-start(bf16[256,256]{0,1:T(8,128)(2,1)S(1)} %get-tuple-element.93), channel_id=1, source_target_pairs={{0,8},{4,12},{8,16},{12,20},{16,24},{20,28},{1,9},{5,13},{9,17},{1... | collective-permute-start | bytes 393224 | tf_op jit(solution)/shard_map/ppermute | solution.py:19
  17.4 1.5 collective-permute-start.3
  18.9 3.9 %collective-permute-start = (bf16[256,256]{0,1:T(8,128)(2,1)S(1)}, bf16[256,256]{0,1:T(8,128)(2,1)S(1)}, u32[]{:S(2)}, u32[]{:S(2)}) collective-permute-start(bf16[256,256]{0,1:T(8,128)(2,1)S(1)} %get-tuple-element.92), channel_id=1, source_target_pairs={{0,8},{4,12},{8,16},{12,20},{16,24},{20,28},{1,9},{5,13},{9,17},{1... | collective-permute-start | bytes 393224 | tf_op jit(solution)/shard_map/ppermute | solution.py:19
  22.8 3.2 %collective-permute-start.1 = (bf16[256,256]{0,1:T(8,128)(2,1)S(1)}, bf16[256,256]{0,1:T(8,128)(2,1)S(1)}, u32[]{:S(2)}, u32[]{:S(2)}) collective-permute-start(bf16[256,256]{0,1:T(8,128)(2,1)S(1)} %get-tuple-element.92), channel_id=1, source_target_pairs={{0,4},{4,8},{8,12},{12,16},{16,20},{20,24},{24,28},{1,5},{5,9},{9,... | collective-permute-start | bytes 393224 | tf_op jit(solution)/shard_map/ppermute | solution.py:19
  26.0 0.2 and_and_fusion
  26.3 0.6 fusion.64
  26.9 1.8 fusion.112
  28.8 0.7 fusion.32
  29.6 0.3 copy-done.3
  29.8 1.4 fusion.119
  31.3 0.5 all-gather.5.cloned.1.call-update
  31.9 1.3 collective-permute-start.4
  34.0 0.6 dynamic-slice
  34.5 0.7 dynamic-update-slice
  35.3 9.8 %all-reduce = s32[8]{0:T(128)S(1)} all-reduce(s32[8]{0:T(128)S(1)} %dynamic-update-slice), channel_id=2, replica_groups=mesh['seq'=8,'tp'=4] {'seq'}, use_global_device_ids=true, to_apply=%add | all-reduce | flops 8 | bytes 64
  45.1 8.7 %while.13 = (s32[]{:T(128)}, s32[1]{0:T(128)}, s32[]{:T(128)}, s32[8,1]{0,1:T(1,128)S(1)}, s32[]{:T(128)}) while((s32[]{:T(128)}, s32[1]{0:T(128)}, s32[]{:T(128)}, s32[8,1]{0,1:T(1,128)S(1)}, s32[]{:T(128)}) %tuple.59), condition=%wide.region_8.9_spmd, body=%wide.region_7.8_spmd.sunk | while | flops 5 | bytes 107 | solution.py:31
  45.1 0.6 constant_dynamic-slice_fusion.2
  46.3 0.6 constant_dynamic-slice_fusion.2
  47.6 0.6 constant_dynamic-slice_fusion.2
  48.8 0.6 constant_dynamic-slice_fusion.2
  50.1 0.6 constant_dynamic-slice_fusion.2
  51.3 0.6 constant_dynamic-slice_fusion.2
  52.6 0.6 constant_dynamic-slice_fusion.2
  54.6 7.3 %all-reduce.1 = s32[512]{0:T(512)S(1)} all-reduce(s32[512]{0:T(512)S(1)} %select_dynamic-update-slice_fusion), channel_id=1, replica_groups=mesh['seq'=8,'tp'=4] {'seq'}, use_global_device_ids=true, to_apply=%add.1 | all-reduce | flops 512 | bytes 4096
  63.3 20.8 %all-reduce.4.cloned.1.call-done = f32[256,1024]{1,0:T(8,128)} async-done(((f32[256,1024]{1,0:T(8,128)}), f32[256,1024]{1,0:T(8,128)}) %all-reduce.4.cloned.1.call-update) | async-done | bytes 1048592 | tf_op jit(solution)/shard_map/psum | solution.py:172
  84.2 1.4 fusion.43
  85.6 1.3 collective-permute-start.5
  86.9 1.8 collective-permute-done.5
  88.7 3.1 %fusion.23 = bf16[33,8,8,128]{3,2,1,0:T(8,128)(2,1)} fusion(bf16[2,1024,1024]{2,1,0:T(8,128)(2,1)} %param.20, bf16[8,1024]{1,0:T(8,128)(2,1)S(1)} %collective-permute-done.5, bf16[256,1024]{1,0:T(8,128)(2,1)S(1)} %fusion.43), kind=kOutput, calls=%fused_computation.30 | convolution fusion | flops 554999808 | bytes 3178496 | tf_op jit(solution)/shard_map/dot_general | solution.py:85
  91.8 0.7 fusion.33
  92.5 2.5 %fusion.113 = (f32[8,64]{1,0:T(8,128)S(1)}, f32[8,64,264]{2,1,0:T(8,128)}) fusion(bf16[33,8,8,128]{3,2,1,0:T(8,128)(2,1)} %fusion.23, pred[64,264]{1,0:T(8,128)(4,1)S(1)} %and_or_fusion, f32[64,1024]{1,0:T(8,128)S(1)} %fusion.33), kind=kOutput, calls=%fused_computation.147 | convolution fusion | flops 35344648 | bytes 1362432 | tf_op jit(solution)/shard_map/sub | solution.py:50
  95.0 2.4 %fusion.26 = bf16[33,8,8,128]{3,2,1,0:T(8,128)(2,1)S(1)} fusion(bf16[2,1024,1024]{2,1,0:T(8,128)(2,1)} %param.20, bf16[8,1024]{1,0:T(8,128)(2,1)S(1)} %collective-permute-done.5, bf16[256,1024]{1,0:T(8,128)(2,1)S(1)} %fusion.43), kind=kOutput, calls=%fused_computation.31 | convolution fusion | flops 554999808 | bytes 3178496 | tf_op jit(solution)/shard_map/dot_general | solution.py:88
  97.4 0.3 convolution_bitcast_fusion.1
  97.8 15.5 %all_gather.27 = bf16[64,4096]{1,0:T(8,128)(2,1)S(1)} all-gather(bf16[64,1024]{1,0:T(8,128)(2,1)S(1)} %fusion.73), channel_id=1, replica_groups=mesh['seq'=8,'tp'=4] {'tp'}, dimensions={1}, use_global_device_ids=true | all-gather | bytes 655360 | tf_op jit(solution)/shard_map/all_gather | solution.py:188
  113.2 0.2 fusion.37
  113.5 7.5 %convolution_bitcast_fusion = f32[3,64,512]{2,1,0:T(8,128)S(1)} fusion(bf16[3,4096,512]{2,1,0:T(8,128)(2,1)} %all-gather.5.cloned.1.call-done, bf16[64,4096]{1,0:T(8,128)(2,1)S(1)} %all_gather.27, f32[4096]{0:T(1024)S(1)} %convert_element_type.118, f32[64]{0:T(128)S(1)} %add_rsqrt_fusion.1), kind=kOutput, calls=%fused_computation.35 | convolution fusion | flops 806354944 | bytes 13517056 | tf_op jit(solution)/shard_map/pd,idc->ipc/dot_general | solution.py:193
  121.6 11.9 %all_gather.29 = bf16[512,512]{1,0:T(8,128)(2,1)S(1)} all-gather(bf16[64,512]{1,0:T(8,128)(2,1)S(1)} %copy_bitcast_fusion), channel_id=1, replica_groups=mesh['seq'=8,'tp'=4] {'seq'}, dimensions={0}, use_global_device_ids=true | all-gather | bytes 589824 | tf_op jit(solution)/shard_map/all_gather | solution.py:211
  133.7 11.9 %all-gather.1 = bf16[1,512,512]{2,1,0:T(8,128)(2,1)S(1)} all-gather(bf16[1,64,512]{2,1,0:T(8,128)(2,1)S(1)} %slice.101), channel_id=3, replica_groups=mesh['seq'=8,'tp'=4] {'seq'}, dimensions={1}, use_global_device_ids=true | all-gather | bytes 589824 | tf_op jit(solution)/shard_map/all_gather | solution.py:212
  145.6 0.9 reshape.384
  146.5 0.4 fusion.118
  146.9 0.2 fusion.57
  147.1 1.3 fusion.36
  148.5 4.0 %fusion.80 = f32[64,4096]{1,0:T(8,128)} fusion(bf16[512,4096]{1,0:T(8,128)(2,1)} %all-gather.7.cloned.1.call-done, bf16[4,8,8,128]{3,2,1,0:T(8,128)(2,1)S(1)} %fusion.36), kind=kOutput, calls=%fused_computation.100 | convolution fusion | flops 268435456 | bytes 5308416 | tf_op jit(solution)/shard_map/dot_general | solution.py:239
  152.6 26.7 %reduce-scatter.2.cloned.1.call-done = f32[64,1024]{1,0:T(8,128)} async-done(((f32[64,4096]{1,0:T(8,128)}), f32[64,1024]{1,0:T(8,128)}) %reduce-scatter.2.cloned.1.call-update) | async-done | bytes 262160 | tf_op jit(solution)/shard_map/reduce_scatter | solution.py:244
  179.3 1.7 select_convert_fusion
  (65 shorter events, 2.1 us)
Async XLA Ops:
  8.0 83.8 %copy-start = (bf16[1024,1024]{1,0:T(8,128)(2,1)S(1)}, bf16[1024,1024]{1,0:T(8,128)(2,1)}, u32[]{:S(2)}) copy-start(bf16[1024,1024]{1,0:T(8,128)(2,1)} %param.19) | copy-start | bytes 6291460
  8.0 76.1 %all-reduce.4.cloned.1.call-start = ((), (), s32[]{:S(2)}) async-start(), calls=%async_computation.1 | async-start | bytes 2097152 | tf_op jit(solution)/shard_map/psum | solution.py:172
  12.5 13.8 %collective-permute-start.2 = (bf16[256,256]{0,1:T(8,128)(2,1)S(1)}, bf16[256,256]{0,1:T(8,128)(2,1)S(1)}, u32[]{:S(2)}, u32[]{:S(2)}) collective-permute-start(bf16[256,256]{0,1:T(8,128)(2,1)S(1)} %get-tuple-element.93), channel_id=1, source_target_pairs={{0,8},{4,12},{8,16},{12,20},{16,24},{20,28},{1,9},{5,13},{9,17},{1... | collective-permute-start | bytes 393224 | tf_op jit(solution)/shard_map/ppermute | solution.py:19
  17.4 8.9 %collective-permute-start.3 = (bf16[256,256]{0,1:T(8,128)(2,1)S(1)}, bf16[256,256]{0,1:T(8,128)(2,1)S(1)}, u32[]{:S(2)}, u32[]{:S(2)}) collective-permute-start(bf16[256,256]{0,1:T(8,128)(2,1)S(1)} %get-tuple-element.93), channel_id=1, source_target_pairs={{0,4},{4,8},{8,12},{12,16},{16,20},{20,24},{24,28},{1,5},{5,9},{9,... | collective-permute-start | bytes 393224 | tf_op jit(solution)/shard_map/ppermute | solution.py:19
  18.9 9.9 %collective-permute-start = (bf16[256,256]{0,1:T(8,128)(2,1)S(1)}, bf16[256,256]{0,1:T(8,128)(2,1)S(1)}, u32[]{:S(2)}, u32[]{:S(2)}) collective-permute-start(bf16[256,256]{0,1:T(8,128)(2,1)S(1)} %get-tuple-element.92), channel_id=1, source_target_pairs={{0,8},{4,12},{8,16},{12,20},{16,24},{20,28},{1,9},{5,13},{9,17},{1... | collective-permute-start | bytes 393224 | tf_op jit(solution)/shard_map/ppermute | solution.py:19
  22.8 6.0 %collective-permute-start.1 = (bf16[256,256]{0,1:T(8,128)(2,1)S(1)}, bf16[256,256]{0,1:T(8,128)(2,1)S(1)}, u32[]{:S(2)}, u32[]{:S(2)}) collective-permute-start(bf16[256,256]{0,1:T(8,128)(2,1)S(1)} %get-tuple-element.92), channel_id=1, source_target_pairs={{0,4},{4,8},{8,12},{12,16},{16,20},{20,24},{24,28},{1,5},{5,9},{9,... | collective-permute-start | bytes 393224 | tf_op jit(solution)/shard_map/ppermute | solution.py:19
  28.8 1.0 copy-start.3
  29.5 2.3 %copy-start.5 = (s32[1,64]{1,0:T(1,128)S(1)}, s32[1,64]{1,0:T(1,128)}, u32[]{:S(2)}) copy-start(s32[1,64]{1,0:T(1,128)} %param.17) | copy-start | bytes 772
  29.5 4.4 %copy-start.6 = (u32[32]{0:T(128)S(1)}, u32[32]{0:T(128)}, u32[]{:S(2)}) copy-start(u32[32]{0:T(128)} %constant.80) | copy-start | bytes 388
  29.5 25.0 %copy-start.4 = (bf16[4096]{0:T(1024)(128)(2,1)S(1)}, bf16[4096]{0:T(1024)(128)(2,1)}, u32[]{:S(2)}) copy-start(bf16[4096]{0:T(1024)(128)(2,1)} %param.21) | copy-start | bytes 24580
  29.5 54.6 %copy-start.1 = (bf16[256,1024]{1,0:T(8,128)(2,1)S(1)}, bf16[256,1024]{1,0:T(8,128)(2,1)}, u32[]{:S(2)}) copy-start(bf16[256,1024]{1,0:T(8,128)(2,1)} %param.13) | copy-start | bytes 1572868
  31.2 82.3 %all-gather.5.cloned.1.call-start = ((), (), s32[]{:S(2)}) async-start(), calls=%async_computation.2 | async-start | bytes 14155776 | tf_op jit(solution)/shard_map/all_gather | solution.py:196
  31.8 116.7 %all-gather.7.cloned.1.call-start = ((), (), s32[]{:S(2)}) async-start(), calls=%async_computation.3 | async-start | bytes 4718592 | tf_op jit(solution)/shard_map/all_gather | solution.py:241
  31.9 30.4 %collective-permute-start.4 = (bf16[1]{0:T(256)(128)(2,1)}, bf16[1]{0:T(256)(128)(2,1)}, u32[]{:S(2)}, u32[]{:S(2)}) collective-permute-start(bf16[1]{0:T(256)(128)(2,1)} %convert_element_type.108), channel_id=1, source_target_pairs={{4,0},{8,4},{12,8},{16,12},{20,16},{24,20},{28,24},{5,1},{9,5},{13... | collective-permute-start | bytes 14 | tf_op jit(solution)/shard_map/ppermute | solution.py:19
  33.2 146.0 %reduce-scatter.2.cloned.1.call-start = ((), (), s32[]{:S(2)}) async-start(), calls=%async_computation.4 | async-start | bytes 1310720 | tf_op jit(solution)/shard_map/reduce_scatter | solution.py:244
  85.5 9.4 %copy-start.2 = (bf16[256,1024]{1,0:T(8,128)(2,1)}, bf16[256,1024]{1,0:T(8,128)(2,1)S(1)}, u32[]{:S(2)}) copy-start(bf16[256,1024]{1,0:T(8,128)(2,1)S(1)} %fusion.43) | copy-start | bytes 1572868
  85.6 3.1 %collective-permute-start.5 = (bf16[8,1024]{1,0:T(8,128)(2,1)S(1)}, bf16[8,1024]{1,0:T(8,128)(2,1)S(1)}, u32[]{:S(2)}, u32[]{:S(2)}) collective-permute-start(bf16[8,1024]{1,0:T(8,128)(2,1)S(1)} %slice.73), channel_id=1, source_target_pairs={{4,0},{8,4},{12,8},{16,12},{20,16},{24,20},{28,24},{5,1},{9,5},{13... | collective-permute-start | bytes 49160 | tf_op jit(solution)/shard_map/ppermute | solution.py:19
  95.0 2.4 %copy-start.7 = (f32[8,64,264]{2,1,0:T(8,128)S(1)}, f32[8,64,264]{2,1,0:T(8,128)}, u32[]{:S(2)}) copy-start(f32[8,64,264]{2,1,0:T(8,128)} %get-tuple-element.112) | copy-start | bytes 1622020
Sparse Core Ops, SparseCore 0:
  31.3 52.7 all-reduce.3
  152.7 26.5 reduce-scatter.1
Sparse Core Ops, SparseCore 1:
  33.6 72.8 all-gather.4
  108.2 39.8 all-gather.6
where the time goes:
time: 189 us; the launch traced here: 188 us
  blocking collectives  56.4 us (30%)
  waiting for transfers between devices  50 us (26%)
  matrix products  27.2 us (14%)
  between operations  17.9 us (9%)
  starting transfers between devices  16.2 us (9%)
  other arithmetic  8.76 us (5%)
  local copies, waits for them, and re-layouts  7.47 us (4%)
  loops' own time  4.55 us (2%)
    reduce_scatter x1, waiting for transfers between devices, shards(): reduced = lax.psum_scatter(partials, 'tp', scatter_dimension=1, tiled=True)  26.7 us
    psum x1, waiting for transfers between devices, shards(): lax.psum(jnp.dot(attended, enc_proj_out, preferred_element_type=jnp.float...  20.8 us
    unnamed x2, blocking collectives  17.1 us
    ppermute x6, starting transfers between devices, from_behind(): lax.ppermute(value, axis, [(source, source + steps) for source in range(l...  16 us
    all_gather x1, blocking collectives, shards(): full_rows = lax.all_gather(patches, 'tp', axis=1, tiled=True)  15.5 us
    all_gather x1, blocking collectives, shards(): piece_keys = lax.all_gather(latent_keys, 'seq', axis=0, tiled=True)  11.9 us
    all_gather x1, blocking collectives, shards(): piece_values = lax.all_gather(latent_values, 'seq', axis=0, tiled=True)  11.9 us
    dot_general x1, matrix products, shards(): jnp.einsum('pd,idc->ipc', normed_rows, lax.all_gather(lat_qkv, 'seq', axi...  7.47 us
  transfers between devices with their start and end apart: 10, of which 3 were waited for; matrix products, arithmetic and copies ran while one was open for 16% of the time, Pallas kernels for 0%

commit v1 on v0

--- a/solution.py
+++ b/solution.py
@@ -208,8 +208,13 @@
     latent_values = projected[2].astype(jnp.bfloat16)
     latent_pos = jnp.where(in_use, position, far_position)
     largest = jnp.full((heads_here, slot_total), -1e30, jnp.float32)
-    piece_keys = lax.all_gather(latent_keys, "seq", axis=0, tiled=True)
-    piece_values = lax.all_gather(latent_values, "seq", axis=0, tiled=True)
+    piece_keys, piece_values = jnp.split(
+        lax.all_gather(
+            jnp.concatenate([latent_keys, latent_values], axis=1), "seq", axis=0, tiled=True
+        ),
+        [latent_keys.shape[1]],
+        axis=1,
+    )
     piece_pos = lax.all_gather(shortened(latent_pos), "seq", axis=0, tiled=True)
     rows_here = piece_keys.shape[0]
     piece_scores = jnp.einsum(

time: 189 us -> 226 us (1.20)
  waiting for transfers between devices: 50 us -> 109 us
  blocking collectives: 56.4 us -> 34.6 us
    all_gather x1, waiting for transfers between devices: 0.03 us -> 36.7 us  [shards(): lax.all_gather(lat_proj_out, 'seq', axis=1, tiled=True)]
    all_gather x2 -> x0, blocking collectives: 23.8 us -> none  [the longest x1 11.9 us: shards(): piece_keys = lax.all_gather(latent_keys, 'seq', axis=0, tiled=True)]
    all_gather x0 -> x1, waiting for transfers between devices: none -> 13.2 us  [shards(): lax.all_gather(jnp.concatenate([latent_keys, latent_values], axis=1), 'se...]
    psum x1, waiting for transfers between devices: 20.8 us -> 28.6 us  [shards(): lax.psum(jnp.dot(attended, enc_proj_out, preferred_element_type=jnp.float...]
  transfers between devices with their start and end apart: 10 -> 11, of which waited for: 3 -> 5; matrix products, arithmetic and copies ran while one was open for 16% -> 10% of each run, Pallas kernels for 0% -> 0%
where the time goes in v1:
time: 226 us; the launch traced here: 225 us
  waiting for transfers between devices  109 us (48%)
  blocking collectives  34.6 us (15%)
  matrix products  25.6 us (11%)
  between operations  18.2 us (8%)
  starting transfers between devices  16.2 us (7%)
  other arithmetic  9.41 us (4%)
  local copies, waits for them, and re-layouts  8.02 us (4%)
  loops' own time  4.56 us (2%)
    all_gather x1, waiting for transfers between devices, shards(): lax.all_gather(lat_proj_out, 'seq', axis=1, tiled=True)  36.7 us
    psum x1, waiting for transfers between devices, shards(): lax.psum(jnp.dot(attended, enc_proj_out, preferred_element_type=jnp.float...  28.6 us
    reduce_scatter x1, waiting for transfers between devices, shards(): reduced = lax.psum_scatter(partials, 'tp', scatter_dimension=1, tiled=True)  27.4 us
    unnamed x2, blocking collectives  19.2 us
    ppermute x6, starting transfers between devices, from_behind(): lax.ppermute(value, axis, [(source, source + steps) for source in range(l...  16 us
    all_gather x1, blocking collectives, shards(): full_rows = lax.all_gather(patches, 'tp', axis=1, tiled=True)  15.4 us
    all_gather x1, waiting for transfers between devices, shards(): lax.all_gather(jnp.concatenate([latent_keys, latent_values], axis=1), 'se...  13.2 us
    dot_general x1, matrix products, shards(): jnp.einsum('pd,idc->ipc', normed_rows, lax.all_gather(lat_qkv, 'seq', axi...  6.93 us
  transfers between devices with their start and end apart: 11, of which 5 were waited for; matrix products, arithmetic and copies ran while one was open for 10% of the time, Pallas kernels for 0%

profile of v1, /device:TPU:0, one launch (start us, length us, event | category | flops | bytes accessed | tf_op | source)
XLA Modules:
  0.0 225.4 jit_solution(2324872350766350450)
XLA Ops:
  8.1 0.8 convert_element_type.99
  8.9 1.2 fusion.40
  10.1 2.4 %fusion.30 = bf16[3,256,256]{1,2,0:T(8,128)(2,1)S(1)} fusion(bf16[3,1024,256]{2,1,0:T(8,128)(2,1)} %param.15, bf16[256,1024]{1,0:T(8,128)(2,1)} %param.13, f32[1024]{0:T(1024)S(1)} %convert_element_type.99, f32[256]{0:T(256)S(1)} %add_rsqrt_fusion), kind=kOutput, calls=%fused_computation.34 | convolution fusion | flops 403898368 | bytes 2495488 | tf_op jit(solution)/shard_map/bd,idc->ibc/dot_general | solution.py:133
  12.5 4.9 %collective-permute-start.2 = (bf16[256,256]{0,1:T(8,128)(2,1)S(1)}, bf16[256,256]{0,1:T(8,128)(2,1)S(1)}, u32[]{:S(2)}, u32[]{:S(2)}) collective-permute-start(bf16[256,256]{0,1:T(8,128)(2,1)S(1)} %get-tuple-element.95), channel_id=1, source_target_pairs={{0,8},{4,12},{8,16},{12,20},{16,24},{20,28},{1,9},{5,13},{9,17},{1... | collective-permute-start | bytes 393224 | tf_op jit(solution)/shard_map/ppermute | solution.py:19
  17.4 1.5 collective-permute-start.3
  18.9 3.9 %collective-permute-start = (bf16[256,256]{0,1:T(8,128)(2,1)S(1)}, bf16[256,256]{0,1:T(8,128)(2,1)S(1)}, u32[]{:S(2)}, u32[]{:S(2)}) collective-permute-start(bf16[256,256]{0,1:T(8,128)(2,1)S(1)} %get-tuple-element.94), channel_id=1, source_target_pairs={{0,8},{4,12},{8,16},{12,20},{16,24},{20,28},{1,9},{5,13},{9,17},{1... | collective-permute-start | bytes 393224 | tf_op jit(solution)/shard_map/ppermute | solution.py:19
  22.8 3.2 %collective-permute-start.1 = (bf16[256,256]{0,1:T(8,128)(2,1)S(1)}, bf16[256,256]{0,1:T(8,128)(2,1)S(1)}, u32[]{:S(2)}, u32[]{:S(2)}) collective-permute-start(bf16[256,256]{0,1:T(8,128)(2,1)S(1)} %get-tuple-element.94), channel_id=1, source_target_pairs={{0,4},{4,8},{8,12},{12,16},{16,20},{20,24},{24,28},{1,5},{5,9},{9,... | collective-permute-start | bytes 393224 | tf_op jit(solution)/shard_map/ppermute | solution.py:19
  26.0 0.2 and_and_fusion
  26.3 0.6 fusion.67
  26.9 1.8 fusion.116
  28.8 0.7 fusion.32
  29.6 0.3 copy-done.3
  29.8 1.3 fusion.123
  31.2 0.5 all-gather.5.cloned.1.call-update
  32.5 0.7 dynamic-slice
  33.2 0.8 dynamic-update-slice
  34.0 1.3 collective-permute-start.4
  35.3 9.8 %all-reduce = s32[8]{0:T(128)S(1)} all-reduce(s32[8]{0:T(128)S(1)} %dynamic-update-slice), channel_id=2, replica_groups=mesh['seq'=8,'tp'=4] {'seq'}, use_global_device_ids=true, to_apply=%add | all-reduce | flops 8 | bytes 64
  45.1 9.0 %while.13 = (s32[]{:T(128)}, s32[1]{0:T(128)}, s32[]{:T(128)}, s32[8,1]{0,1:T(1,128)S(1)}, s32[]{:T(128)}) while((s32[]{:T(128)}, s32[1]{0:T(128)}, s32[]{:T(128)}, s32[8,1]{0,1:T(1,128)S(1)}, s32[]{:T(128)}) %tuple.62), condition=%wide.region_8.9_spmd, body=%wide.region_7.8_spmd.sunk | while | flops 5 | bytes 107 | solution.py:31
  45.1 0.6 constant_dynamic-slice_fusion.2
  46.4 0.6 constant_dynamic-slice_fusion.2
  47.7 0.6 constant_dynamic-slice_fusion.2
  49.0 0.6 constant_dynamic-slice_fusion.2
  50.3 0.6 constant_dynamic-slice_fusion.2
  51.5 0.6 constant_dynamic-slice_fusion.2
  52.8 0.6 constant_dynamic-slice_fusion.2
  55.5 28.6 %all-reduce.4.cloned.1.call-done = f32[256,1024]{1,0:T(8,128)} async-done(((f32[256,1024]{1,0:T(8,128)}), f32[256,1024]{1,0:T(8,128)}) %all-reduce.4.cloned.1.call-update) | async-done | bytes 1048592 | tf_op jit(solution)/shard_map/psum | solution.py:172
  84.1 1.4 fusion.43
  85.5 1.3 collective-permute-start.5
  86.8 1.8 collective-permute-done.5
  88.6 3.1 %fusion.23 = bf16[33,8,8,128]{3,2,1,0:T(8,128)(2,1)} fusion(bf16[2,1024,1024]{2,1,0:T(8,128)(2,1)} %param.20, bf16[8,1024]{1,0:T(8,128)(2,1)S(1)} %collective-permute-done.5, bf16[256,1024]{1,0:T(8,128)(2,1)S(1)} %fusion.43), kind=kOutput, calls=%fused_computation.30 | convolution fusion | flops 554999808 | bytes 3178496 | tf_op jit(solution)/shard_map/dot_general | solution.py:85
  91.7 0.7 fusion.33
  92.4 2.5 %fusion.117 = (f32[8,64]{1,0:T(8,128)S(1)}, f32[8,64,264]{2,1,0:T(8,128)}) fusion(bf16[33,8,8,128]{3,2,1,0:T(8,128)(2,1)} %fusion.23, pred[64,264]{1,0:T(8,128)(4,1)S(1)} %and_or_fusion, f32[64,1024]{1,0:T(8,128)S(1)} %fusion.33), kind=kOutput, calls=%fused_computation.154 | convolution fusion | flops 35344648 | bytes 1362432 | tf_op jit(solution)/shard_map/sub | solution.py:50
  94.9 2.4 %fusion.26 = bf16[33,8,8,128]{3,2,1,0:T(8,128)(2,1)S(1)} fusion(bf16[2,1024,1024]{2,1,0:T(8,128)(2,1)} %param.20, bf16[8,1024]{1,0:T(8,128)(2,1)S(1)} %collective-permute-done.5, bf16[256,1024]{1,0:T(8,128)(2,1)S(1)} %fusion.43), kind=kOutput, calls=%fused_computation.31 | convolution fusion | flops 554999808 | bytes 3178496 | tf_op jit(solution)/shard_map/dot_general | solution.py:88
  97.3 0.3 convolution_bitcast_fusion.1
  97.7 15.4 %all_gather.24 = bf16[64,4096]{1,0:T(8,128)(2,1)S(1)} all-gather(bf16[64,1024]{1,0:T(8,128)(2,1)S(1)} %fusion.76), channel_id=1, replica_groups=mesh['seq'=8,'tp'=4] {'tp'}, dimensions={1}, use_global_device_ids=true | all-gather | bytes 655360 | tf_op jit(solution)/shard_map/all_gather | solution.py:188
  113.4 6.9 %convolution_bitcast_fusion = f32[3,64,512]{2,1,0:T(8,128)S(1)} fusion(bf16[3,4096,512]{2,1,0:T(8,128)(2,1)} %all-gather.5.cloned.1.call-done, bf16[64,4096]{1,0:T(8,128)(2,1)S(1)} %all_gather.24, f32[4096]{0:T(1024)S(1)} %convert_element_type.118, f32[64]{0:T(128)S(1)} %add_rsqrt_fusion.1), kind=kOutput, calls=%fused_computation.35 | convolution fusion | flops 806354944 | bytes 13517056 | tf_op jit(solution)/shard_map/pd,idc->ipc/dot_general | solution.py:193
  120.9 0.7 pad_maximum_fusion.5
  121.7 0.5 all-gather.9.cloned.1.call-update
  123.0 9.4 %all-reduce.1 = s32[512]{0:T(512)S(1)} all-reduce(s32[512]{0:T(512)S(1)} %select_dynamic-update-slice_fusion), channel_id=1, replica_groups=mesh['seq'=8,'tp'=4] {'seq'}, use_global_device_ids=true, to_apply=%add.1 | all-reduce | flops 512 | bytes 4096
  132.5 13.2 %all-gather.7.cloned.1.call-done = bf16[512,1024]{1,0:T(8,128)(2,1)} async-done(((bf16[64,1024]{1,0:T(8,128)(2,1)}), bf16[512,1024]{1,0:T(8,128)(2,1)}) %all-gather.7.cloned.1.call-update) | async-done | bytes 1048592 | tf_op jit(solution)/shard_map/all_gather | solution.py:212
  145.7 1.3 slice_bitcast_fusion.1
  147.0 0.4 fusion.122
  147.6 0.3 fusion.36
  148.0 36.7 %all-gather.9.cloned.1.call-done = bf16[512,4096]{1,0:T(8,128)(2,1)} async-done(((bf16[512,512]{1,0:T(8,128)(2,1)}), bf16[512,4096]{1,0:T(8,128)(2,1)}) %all-gather.9.cloned.1.call-update) | async-done | bytes 4194320 | tf_op jit(solution)/shard_map/all_gather | solution.py:246
  184.7 4.0 %fusion.84 = f32[64,4096]{1,0:T(8,128)} fusion(bf16[512,4096]{1,0:T(8,128)(2,1)} %all-gather.9.cloned.1.call-done, bf16[4,8,8,128]{3,2,1,0:T(8,128)(2,1)S(1)} %fusion.36), kind=kOutput, calls=%fused_computation.107 | convolution fusion | flops 268435456 | bytes 5308416 | tf_op jit(solution)/shard_map/dot_general | solution.py:244
  188.7 27.4 %reduce-scatter.2.cloned.1.call-done = f32[64,1024]{1,0:T(8,128)} async-done(((f32[64,4096]{1,0:T(8,128)}), f32[64,1024]{1,0:T(8,128)}) %reduce-scatter.2.cloned.1.call-update) | async-done | bytes 262160 | tf_op jit(solution)/shard_map/reduce_scatter | solution.py:249
  216.2 1.7 select_convert_fusion
  (66 shorter events, 2.4 us)
Async XLA Ops:
  8.0 83.8 %copy-start = (bf16[1024,1024]{1,0:T(8,128)(2,1)S(1)}, bf16[1024,1024]{1,0:T(8,128)(2,1)}, u32[]{:S(2)}) copy-start(bf16[1024,1024]{1,0:T(8,128)(2,1)} %param.19) | copy-start | bytes 6291460
  8.0 76.1 %all-reduce.4.cloned.1.call-start = ((), (), s32[]{:S(2)}) async-start(), calls=%async_computation.1 | async-start | bytes 2097152 | tf_op jit(solution)/shard_map/psum | solution.py:172
  12.5 13.8 %collective-permute-start.2 = (bf16[256,256]{0,1:T(8,128)(2,1)S(1)}, bf16[256,256]{0,1:T(8,128)(2,1)S(1)}, u32[]{:S(2)}, u32[]{:S(2)}) collective-permute-start(bf16[256,256]{0,1:T(8,128)(2,1)S(1)} %get-tuple-element.95), channel_id=1, source_target_pairs={{0,8},{4,12},{8,16},{12,20},{16,24},{20,28},{1,9},{5,13},{9,17},{1... | collective-permute-start | bytes 393224 | tf_op jit(solution)/shard_map/ppermute | solution.py:19
  17.4 8.9 %collective-permute-start.3 = (bf16[256,256]{0,1:T(8,128)(2,1)S(1)}, bf16[256,256]{0,1:T(8,128)(2,1)S(1)}, u32[]{:S(2)}, u32[]{:S(2)}) collective-permute-start(bf16[256,256]{0,1:T(8,128)(2,1)S(1)} %get-tuple-element.95), channel_id=1, source_target_pairs={{0,4},{4,8},{8,12},{12,16},{16,20},{20,24},{24,28},{1,5},{5,9},{9,... | collective-permute-start | bytes 393224 | tf_op jit(solution)/shard_map/ppermute | solution.py:19
  18.9 9.9 %collective-permute-start = (bf16[256,256]{0,1:T(8,128)(2,1)S(1)}, bf16[256,256]{0,1:T(8,128)(2,1)S(1)}, u32[]{:S(2)}, u32[]{:S(2)}) collective-permute-start(bf16[256,256]{0,1:T(8,128)(2,1)S(1)} %get-tuple-element.94), channel_id=1, source_target_pairs={{0,8},{4,12},{8,16},{12,20},{16,24},{20,28},{1,9},{5,13},{9,17},{1... | collective-permute-start | bytes 393224 | tf_op jit(solution)/shard_map/ppermute | solution.py:19
  22.8 6.0 %collective-permute-start.1 = (bf16[256,256]{0,1:T(8,128)(2,1)S(1)}, bf16[256,256]{0,1:T(8,128)(2,1)S(1)}, u32[]{:S(2)}, u32[]{:S(2)}) collective-permute-start(bf16[256,256]{0,1:T(8,128)(2,1)S(1)} %get-tuple-element.94), channel_id=1, source_target_pairs={{0,4},{4,8},{8,12},{12,16},{16,20},{20,24},{24,28},{1,5},{5,9},{9,... | collective-permute-start | bytes 393224 | tf_op jit(solution)/shard_map/ppermute | solution.py:19
  28.8 1.0 copy-start.3
  29.5 2.3 %copy-start.5 = (s32[1,64]{1,0:T(1,128)S(1)}, s32[1,64]{1,0:T(1,128)}, u32[]{:S(2)}) copy-start(s32[1,64]{1,0:T(1,128)} %param.17) | copy-start | bytes 772
  29.5 3.0 %copy-start.6 = (u32[32]{0:T(128)S(1)}, u32[32]{0:T(128)}, u32[]{:S(2)}) copy-start(u32[32]{0:T(128)} %constant.80) | copy-start | bytes 388
  29.5 15.6 %copy-start.4 = (bf16[4096]{0:T(1024)(128)(2,1)S(1)}, bf16[4096]{0:T(1024)(128)(2,1)}, u32[]{:S(2)}) copy-start(bf16[4096]{0:T(1024)(128)(2,1)} %param.21) | copy-start | bytes 24580
  29.5 54.6 %copy-start.1 = (bf16[256,1024]{1,0:T(8,128)(2,1)S(1)}, bf16[256,1024]{1,0:T(8,128)(2,1)}, u32[]{:S(2)}) copy-start(bf16[256,1024]{1,0:T(8,128)(2,1)} %param.13) | copy-start | bytes 1572868
  31.2 82.2 %all-gather.5.cloned.1.call-start = ((), (), s32[]{:S(2)}) async-start(), calls=%async_computation.2 | async-start | bytes 14155776 | tf_op jit(solution)/shard_map/all_gather | solution.py:196
  31.7 114.0 %all-gather.7.cloned.1.call-start = ((), (), s32[]{:S(2)}) async-start(), calls=%async_computation.3 | async-start | bytes 1179648 | tf_op jit(solution)/shard_map/all_gather | solution.py:212
  34.0 20.5 %collective-permute-start.4 = (bf16[1]{0:T(256)(128)(2,1)}, bf16[1]{0:T(256)(128)(2,1)}, u32[]{:S(2)}, u32[]{:S(2)}) collective-permute-start(bf16[1]{0:T(256)(128)(2,1)} %convert_element_type.108), channel_id=1, source_target_pairs={{4,0},{8,4},{12,8},{16,12},{20,16},{24,20},{28,24},{5,1},{9,5},{13... | collective-permute-start | bytes 14 | tf_op jit(solution)/shard_map/ppermute | solution.py:19
  85.5 9.4 %copy-start.2 = (bf16[256,1024]{1,0:T(8,128)(2,1)}, bf16[256,1024]{1,0:T(8,128)(2,1)S(1)}, u32[]{:S(2)}) copy-start(bf16[256,1024]{1,0:T(8,128)(2,1)S(1)} %fusion.43) | copy-start | bytes 1572868
  85.5 3.1 %collective-permute-start.5 = (bf16[8,1024]{1,0:T(8,128)(2,1)S(1)}, bf16[8,1024]{1,0:T(8,128)(2,1)S(1)}, u32[]{:S(2)}, u32[]{:S(2)}) collective-permute-start(bf16[8,1024]{1,0:T(8,128)(2,1)S(1)} %slice.73), channel_id=1, source_target_pairs={{4,0},{8,4},{12,8},{16,12},{20,16},{24,20},{28,24},{5,1},{9,5},{13... | collective-permute-start | bytes 49160 | tf_op jit(solution)/shard_map/ppermute | solution.py:19
  94.9 2.4 %copy-start.7 = (f32[8,64,264]{2,1,0:T(8,128)S(1)}, f32[8,64,264]{2,1,0:T(8,128)}, u32[]{:S(2)}) copy-start(f32[8,64,264]{2,1,0:T(8,128)} %get-tuple-element.114) | copy-start | bytes 1622020
  121.6 63.1 %all-gather.9.cloned.1.call-start = ((), (), s32[]{:S(2)}) async-start(), calls=%async_computation.4 | async-start | bytes 4718592 | tf_op jit(solution)/shard_map/all_gather | solution.py:246
  122.2 94.0 %reduce-scatter.2.cloned.1.call-start = ((), (), s32[]{:S(2)}) async-start(), calls=%async_computation.5 | async-start | bytes 1310720 | tf_op jit(solution)/shard_map/reduce_scatter | solution.py:249
Sparse Core Ops, SparseCore 0:
  31.3 52.7 all-reduce.3
  188.8 27.2 reduce-scatter.1
Sparse Core Ops, SparseCore 1:
  33.6 72.7 all-gather.4
  121.7 23.9 all-gather.6
  147.4 37.2 all-gather.8
